TPU v7x, 32 devices: a whole 2x2x4 slice. The times are simulated.
32 devices in a mesh: dp: 8 (over z, core), mp: 4 (over y, x).
Axes of the slice: x: 2, y: 2, z: 4, core: 2. Of those that a mesh axis runs over, the one named last changes fastest.
Arguments:
- inputs: bfloat16 [1024, 32768], P('dp', 'mp'), may hold values from -6 to 6
- cotangent: bfloat16 [1024, 32768], P('dp', 'mp'), may hold values from -6 to 6
- first_weight: bfloat16 [128, 2, 256, 256], P('mp', None, 'dp'), may hold values from -0.25 to 0.25
- second_weight: bfloat16 [128, 2, 256, 256], P('mp', None, 'dp'), may hold values from -0.25 to 0.25
- orders: int32 [2, 256], replicated, may hold values from 0 to 255, each once within a row
Outputs:
- input_grad: bfloat16 [1024, 32768], P('dp', 'mp')
- first_grad: float32 [128, 2, 256, 256], P('mp', None, 'dp')
- second_grad: float32 [128, 2, 256, 256], P('mp', None, 'dp')
Inputs may be any that keep to these rules, and one draw needn't show every extreme that they name: Each of the two rows of orders is a permutation of 0 to 255.
All inputs are finite; a program needn't handle non-finite values.
Results may differ from a plain program's by a relative error of at most 0.018.
Values may be sent and summed in bfloat16 or wider, within the bound.
A program may use at most 128 MiB of HBM per device.

v0:
```python
import math
import jax
import jax.numpy as jnp
from jax import lax
from jax.sharding import PartitionSpec as P

B = 256


def partner(value, axis, bit):
    mask = 2**bit
    pairs = [(source, source ^ mask) for source in range(lax.axis_size(axis))]
    return lax.ppermute(value, axis, pairs)


def gelu_tanh(argument):
    return jax.nn.gelu(argument, approximate=True)


def inverse_order(order):
    length = order.shape[0]
    positions = jnp.arange(length, dtype=jnp.int32)
    matches = order[None, :] == positions[:, None]
    return jnp.sum(jnp.where(matches, positions[None, :], 0), axis=1)


def contract(left, right):
    return jnp.einsum("tnk,nkj->tnj", left, right, preferred_element_type=jnp.float32)


def contract_back(left, right):
    return jnp.einsum("tnj,nkj->tnk", left, right, preferred_element_type=jnp.float32)


def outer_sum(left, right):
    return jnp.einsum("tnk,tnj->nkj", left, right, preferred_element_type=jnp.float32)


def shards(inputs, cotangent, first_weight, second_weight, orders):
    tok_rows = inputs.shape[0]
    feature_width = inputs.shape[1]
    local_blocks = feature_width // B
    bit_top = lax.axis_size("mp").bit_length() - 2
    bit_next = bit_top - 1
    grad_scale = 1.0 / math.sqrt(tok_rows * lax.axis_size("dp"))
    order_first = orders[0]
    order_second = orders[1]
    inverse_first = inverse_order(order_first)
    inverse_second = inverse_order(order_second)
    first_full = lax.all_gather(first_weight, "dp", axis=2, tiled=True)
    own_first = first_full[:, 0]
    cross_first = jnp.take(first_full[:, 1], inverse_first, axis=1)
    blocks_in = inputs.reshape(tok_rows, local_blocks, B)
    partner_in = partner(inputs, "mp", bit_top).reshape(tok_rows, local_blocks, B)
    pre_act = contract(blocks_in, own_first) + contract(partner_in, cross_first)
    saved_pre = pre_act.astype(jnp.bfloat16)
    activated = gelu_tanh(pre_act).astype(jnp.bfloat16)
    blocks_cot = cotangent.reshape(tok_rows, local_blocks, B)
    moved_rows = partner(second_weight[:, 1:], "mp", bit_next)
    held_rows = jnp.concatenate([second_weight[:, :1], moved_rows], axis=1)
    second_full = lax.all_gather(held_rows, "dp", axis=2, tiled=True)
    own_second = second_full[:, 0]
    cross_second = jnp.take(second_full[:, 1], inverse_second, axis=1)
    cot_partner = partner(blocks_cot, "mp", bit_next)
    cross_two = contract_back(cot_partner, cross_second).astype(jnp.bfloat16)
    grad_cross = jnp.take(outer_sum(activated, cot_partner), order_second, axis=1)
    act_grad = contract_back(blocks_cot, own_second) + cross_two.astype(jnp.float32)
    pullback = jax.vjp(gelu_tanh, saved_pre.astype(jnp.float32))[1]
    pre_grad = pullback(act_grad)[0].astype(jnp.bfloat16)
    second_term = jnp.stack([outer_sum(activated, blocks_cot), grad_cross], axis=1) * grad_scale
    product_one = contract_back(pre_grad, cross_first).astype(jnp.bfloat16)
    cross_one = partner(product_one, "mp", bit_top)
    input_grad = (contract_back(pre_grad, own_first) + cross_one.astype(jnp.float32)).astype(
        jnp.bfloat16
    )
    input_grad = input_grad.reshape(tok_rows, feature_width)
    first_cross = jnp.take(outer_sum(partner_in, pre_grad), order_first, axis=1)
    first_term = jnp.stack([outer_sum(blocks_in, pre_grad), first_cross], axis=1) * grad_scale
    first_sum, second_sum = (
        lax.psum_scatter(
            first_term.astype(jnp.bfloat16), "dp", scatter_dimension=2, tiled=True
        ).astype(jnp.float32),
        lax.psum_scatter(
            second_term.astype(jnp.bfloat16), "dp", scatter_dimension=2, tiled=True
        ).astype(jnp.float32),
    )
    returned = partner(second_sum[:, 1:].astype(jnp.bfloat16), "mp", bit_next).astype(jnp.float32)
    second_sum = jnp.concatenate([second_sum[:, :1], returned], axis=1)
    return (input_grad, first_sum, second_sum)


def solution(mesh):
    in_specs = (
        P("dp", "mp"),
        P("dp", "mp"),
        P("mp", None, "dp", None),
        P("mp", None, "dp", None),
        P(),
    )
    out_specs = (P("dp", "mp"), P("mp", None, "dp", None), P("mp", None, "dp", None))
    return jax.shard_map(shards, mesh=mesh, in_specs=in_specs, out_specs=out_specs, check_vma=False)
```

profile of v0, /device:TPU:0, one launch (start us, length us, event | category | flops | bytes accessed | tf_op | source)
XLA Modules:
  0.0 375.4 jit_solution(8754357749359150172)
XLA Ops:
  14.5 11.9 %collective-permute-done = bf16[32,1,32,256]{3,2,0,1:T(8,128)(2,1)S(1)} collective-permute-done((bf16[32,1,32,256]{3,2,0,1:T(8,128)(2,1)S(1)}, bf16[32,1,32,256]{3,2,0,1:T(8,128)(2,1)S(1)}, u32[]{:S(2)}, u32[]{:S(2)}) %collective-permute-start) | collective-permute-done | bytes 524320 | tf_op jit(solution)/shard_map/ppermute | solution.py:13
  39.8 55.3 %all-gather.5.cloned.1.call-done = bf16[32,2,256,256]{3,0,1,2:T(8,128)(2,1)} async-done(((bf16[32,2,32,256]{3,0,1,2:T(8,128)(2,1)}), bf16[32,2,256,256]{3,0,1,2:T(8,128)(2,1)}) %all-gather.5.cloned.1.call-update) | async-done | bytes 8388624 | tf_op jit(solution)/shard_map/all_gather | solution.py:50
  95.1 6.0 %slice_bitcast_fusion = (bf16[32,256,256]{2,0,1:T(8,128)(2,1)}, bf16[32,1,256,256]{3,0,1,2:T(8,128)(2,1)}) fusion(bf16[32,2,256,256]{3,0,1,2:T(8,128)(2,1)} %all-gather.5.cloned.1.call-done), kind=kLoop, calls=%fused_computation.32 | loop fusion | bytes 16777216 | tf_op jit(solution)/shard_map/squeeze | solution.py:52
  101.0 7.8 %copy.130 = bf16[32,1,256,256]{2,3,0,1:T(8,128)(2,1)} copy(bf16[32,1,256,256]{3,0,1,2:T(8,128)(2,1)} %get-tuple-element.18) | data formatting | bytes 8388608
  108.8 5.0 %gather_fusion.1 = bf16[256,32,256]{2,1,0:T(8,128)(2,1)} fusion(bf16[32,256,256]{2,0,1:T(8,128)(2,1)} %get-tuple-element.17, s32[1024]{0:T(1024)S(1)} %pad_clamp_fusion.2), kind=kCustom, calls=%fused_computation.2.clone | custom fusion | bytes 8389632 | tf_op jit(solution)/shard_map/jit(_take)/gather | solution.py:52
  119.4 6.9 %fusion.32 = f32[32,256,128]{2,1,0:T(8,128)S(1)} fusion(f32[32,256,128]{2,1,0:T(8,128)S(1)} %fusion.23, bf16[128,32,256]{0,2,1:T(8,128)(2,1)} %bitcast.10, bf16[32,256,256]{2,0,1:T(8,128)(2,1)S(1)} %select_bitcast_fusion.2), kind=kOutput, calls=%fused_computation.56 | convolution fusion | flops 537919488 | bytes 14680064 | tf_op jit(solution)/shard_map/tnk,nkj->tnj/dot_general | solution.py:28
  131.4 8.3 %copy.112 = f32[32,256,256]{2,0,1:T(8,128)} copy(f32[32,256,256]{2,1,0:T(8,128)S(1)} %fusion.41) | data formatting | bytes 16777216 | tf_op jit(solution)/shard_map/tnk,tnj->nkj/dot_general | solution.py:36
  139.7 7.7 %gather_fusion.3 = f32[256,32,256]{2,1,0:T(8,128)} fusion(f32[32,256,256]{2,0,1:T(8,128)} %copy.112, s32[1024]{0:T(1024)S(1)} %pad_clamp_fusion), kind=kCustom, calls=%fused_computation.3.clone | custom fusion | bytes 16778240 | tf_op jit(solution)/shard_map/jit(_take)/gather | solution.py:66
  147.4 10.0 %copy.113 = f32[256,32,256]{0,2,1:T(8,128)} copy(f32[256,32,256]{2,1,0:T(8,128)} %gather_fusion.3) | data formatting | bytes 16777216 | tf_op jit(solution)/shard_map/jit(_take)/gather | solution.py:66
  165.4 4.4 %fusion.1 = bf16[32,2,256,256]{2,3,0,1:T(8,128)(2,1)} fusion(f32[32,1,256,256]{2,3,0,1:T(8,128)S(1)} %select_bitcast_fusion, f32[32,1,256,256]{2,3,0,1:T(8,128)S(1)} %convolution_bitcast_fusion), kind=kLoop, calls=%fused_computation.7 | loop fusion | flops 12582912 | bytes 25165824 | tf_op jit(solution)/shard_map/convert_element_type | solution.py:84
  169.9 14.6 %copy.114 = bf16[32,2,256,256]{3,0,1,2:T(8,128)(2,1)} copy(bf16[32,2,256,256]{2,3,0,1:T(8,128)(2,1)} %fusion.1) | data formatting | bytes 16777216 | tf_op jit(solution)/shard_map/convert_element_type | solution.py:84
  187.3 4.4 %copy.89 = bf16[32,256,256]{2,0,1:T(8,128)(2,1)} copy(bf16[32,256,256]{2,1,0:T(8,128)(2,1)S(1)} %slice_bitcast_fusion.1) | data formatting | bytes 8388608 | tf_op jit(solution)/shard_map/squeeze | solution.py:63
  191.6 5.0 %gather_fusion = bf16[256,32,256]{2,1,0:T(8,128)(2,1)} fusion(bf16[32,256,256]{2,0,1:T(8,128)(2,1)} %copy.89, s32[1024]{0:T(1024)S(1)} %pad_clamp_fusion.3), kind=kCustom, calls=%fused_computation.clone | custom fusion | bytes 8389632 | tf_op jit(solution)/shard_map/jit(_take)/gather | solution.py:63
  203.9 5.8 %fusion.5 = bf16[128,32,256]{0,2,1:T(8,128)(2,1)S(1)} fusion(f32[32,256,128]{2,1,0:T(8,128)S(1)} %copy-done.1, bf16[32,256,128]{2,1,0:T(8,128)(2,1)S(1)} %fusion.26, bf16[128,32,256]{0,2,1:T(8,128)(2,1)S(1)} %bitcast.87, bf16[32,2,256,256]{3,2,0,1:T(8,128)(2,1)} %all-gather.3.cloned.1.call-done), kind=kOutput, calls=%fused_computation.18 | convolution fusion | flops 562036736 | bytes 14680064 | tf_op jit(solution)/shard_map/tnj,nkj->tnk/dot_general | solution.py:32
  209.7 6.1 %convolution_bitcast_fusion.1 = f32[32,256,256]{1,2,0:T(8,128)} fusion(bf16[128,32,256]{0,2,1:T(8,128)(2,1)S(1)} %fusion.5, bf16[128,32,256]{0,2,1:T(8,128)(2,1)} %bitcast.10), kind=kOutput, calls=%fused_computation.54 | convolution fusion | flops 536870912 | bytes 12582912 | tf_op jit(solution)/shard_map/tnk,tnj->nkj/dot_general | solution.py:36
  215.8 10.3 %copy.107 = f32[32,256,256]{2,0,1:T(8,128)} copy(f32[32,256,256]{1,2,0:T(8,128)} %convolution_bitcast_fusion.1) | data formatting | bytes 16777216 | tf_op jit(solution)/shard_map/tnk,tnj->nkj/dot_general | solution.py:36
  226.2 7.8 %gather_fusion.2 = f32[256,32,256]{2,1,0:T(8,128)} fusion(f32[32,256,256]{2,0,1:T(8,128)} %copy.107, s32[1024]{0:T(1024)S(1)} %pad_clamp_fusion.1), kind=kCustom, calls=%fused_computation.1.clone | custom fusion | bytes 16778240 | tf_op jit(solution)/shard_map/jit(_take)/gather | solution.py:77
  234.0 10.0 %copy.108 = f32[256,32,256]{0,2,1:T(8,128)} copy(f32[256,32,256]{2,1,0:T(8,128)} %gather_fusion.2) | data formatting | bytes 16777216 | tf_op jit(solution)/shard_map/jit(_take)/gather | solution.py:77
  250.9 4.5 %fusion = bf16[32,2,256,256]{2,3,0,1:T(8,128)(2,1)} fusion(f32[32,1,256,256]{2,3,0,1:T(8,128)S(1)} %select_bitcast_fusion.1, f32[32,1,256,256]{2,3,0,1:T(8,128)S(1)} %convolution_bitcast_fusion.2), kind=kLoop, calls=%fused_computation.5 | loop fusion | flops 12582912 | bytes 25165824 | tf_op jit(solution)/shard_map/convert_element_type | solution.py:81
  255.5 14.9 %copy.109 = bf16[32,2,256,256]{3,0,1,2:T(8,128)(2,1)} copy(bf16[32,2,256,256]{2,3,0,1:T(8,128)(2,1)} %fusion) | data formatting | bytes 16777216 | tf_op jit(solution)/shard_map/convert_element_type | solution.py:81
  270.3 6.2 %convert_bitcast_fusion = bf16[128,32,256]{2,0,1:T(8,128)(2,1)} fusion(bf16[128,32,256]{0,2,1:T(8,128)(2,1)S(1)} %fusion.5, bf16[32,256,256]{2,0,1:T(8,128)(2,1)} %copy-done.2), kind=kOutput, calls=%fused_computation.59 | convolution fusion | flops 537919488 | bytes 8388608 | tf_op jit(solution)/shard_map/tnj,nkj->tnk/dot_general | solution.py:32
  281.3 43.4 %collective-permute-done.3 = bf16[128,32,256]{2,0,1:T(8,128)(2,1)} collective-permute-done((bf16[128,32,256]{2,0,1:T(8,128)(2,1)}, bf16[128,32,256]{2,0,1:T(8,128)(2,1)}, u32[]{:S(2)}, u32[]{:S(2)}) %collective-permute-start.3) | collective-permute-done | bytes 2097184 | tf_op jit(solution)/shard_map/ppermute | solution.py:13
  324.6 5.2 %fusion.20 = bf16[128,32,256]{2,0,1:T(8,128)(2,1)} fusion(bf16[128,32,256]{2,0,1:T(8,128)(2,1)} %collective-permute-done.3, bf16[128,32,256]{0,2,1:T(8,128)(2,1)S(1)} %fusion.5, bf16[32,1,256,256]{2,3,0,1:T(8,128)(2,1)} %copy.130), kind=kOutput, calls=%fused_computation.37 | convolution fusion | flops 540016640 | bytes 10485760 | tf_op jit(solution)/shard_map/tnj,nkj->tnk/dot_general | solution.py:32
  336.3 26.7 %reduce-scatter.3.cloned.1.call-done = bf16[32,2,32,256]{3,0,1,2:T(8,128)(2,1)} async-done(((bf16[32,2,256,256]{3,0,1,2:T(8,128)(2,1)}), bf16[32,2,32,256]{3,0,1,2:T(8,128)(2,1)}) %reduce-scatter.3.cloned.1.call-update) | async-done | bytes 1048592 | tf_op jit(solution)/shard_map/reduce_scatter | solution.py:80
  (74 shorter events, 72.9 us)
Async XLA Ops:
  7.2 20.5 %copy-start.6 = (bf16[128,8192]{1,0:T(8,128)(2,1)S(1)}, bf16[128,8192]{1,0:T(8,128)(2,1)}, u32[]{:S(2)}) copy-start(bf16[128,8192]{1,0:T(8,128)(2,1)} %param.9) | copy-start | bytes 6291460
  7.2 87.9 %all-gather.5.cloned.1.call-start = ((), (), s32[]{:S(2)}) async-start(), calls=%async_computation.3 | async-start | bytes 9437184 | tf_op jit(solution)/shard_map/all_gather | solution.py:50
  10.2 174.6 %all-gather.3.cloned.1.call-start = ((), (), s32[]{:S(2)}) async-start(), calls=%async_computation.2 | async-start | bytes 9437184 | tf_op jit(solution)/shard_map/all_gather | solution.py:61
  11.5 15.0 %collective-permute-start = (bf16[32,1,32,256]{3,2,0,1:T(8,128)(2,1)S(1)}, bf16[32,1,32,256]{3,2,0,1:T(8,128)(2,1)S(1)}, u32[]{:S(2)}, u32[]{:S(2)}) collective-permute-start(bf16[32,1,32,256]{3,2,0,1:T(8,128)(2,1)S(1)} %get-tuple-element.22), channel_id=1, source_target_pairs={{0,1},{1,0},{2,3},{3,2},{4,5},{5,4},{6,7},{7,6},{8,9},{9,8},{10,11... | collective-permute-start | bytes 1572872 | tf_op jit(solution)/shard_map/ppermute | solution.py:13
  27.6 250.5 %reduce-scatter.5.cloned.1.call-start = ((), (), s32[]{:S(2)}) async-start(), calls=%async_computation.5 | async-start | bytes 9437184 | tf_op jit(solution)/shard_map/reduce_scatter | solution.py:83
  30.1 9.4 %copy-start.8 = (s32[2,256]{1,0:T(2,128)S(1)}, s32[2,256]{1,0:T(2,128)}, u32[]{:S(2)}) copy-start(s32[2,256]{1,0:T(2,128)} %param.13) | copy-start | bytes 6148
  30.1 89.3 %collective-permute-start.2 = (bf16[128,8192]{0,1:T(8,128)(2,1)}, bf16[128,8192]{0,1:T(8,128)(2,1)}, u32[]{:S(2)}, u32[]{:S(2)}) collective-permute-start(bf16[128,8192]{0,1:T(8,128)(2,1)} %copy.96), channel_id=1, source_target_pairs={{0,2},{1,3},{2,0},{3,1},{4,6},{5,7},{6,4},{7,5},{8,10},{9,11},{10,... | collective-permute-start | bytes 6291464 | tf_op jit(solution)/shard_map/ppermute | solution.py:13
  35.2 122.3 %copy-start.4 = (bf16[128,8192]{0,1:T(8,128)(2,1)}, bf16[128,8192]{0,1:T(8,128)(2,1)S(1)}, u32[]{:S(2)}) copy-start(bf16[128,8192]{0,1:T(8,128)(2,1)S(1)} %copy.87) | copy-start | bytes 6291460
  38.1 88.2 %collective-permute-start.1 = (bf16[128,32,256]{2,0,1:T(8,128)(2,1)}, bf16[128,32,256]{2,0,1:T(8,128)(2,1)}, u32[]{:S(2)}, u32[]{:S(2)}) collective-permute-start(bf16[128,32,256]{2,0,1:T(8,128)(2,1)} %copy.90), channel_id=1, source_target_pairs={{0,1},{1,0},{2,3},{3,2},{4,5},{5,4},{6,7},{7,6},{8,9},{9,8},{10,11... | collective-permute-start | bytes 6291464 | tf_op jit(solution)/shard_map/ppermute | solution.py:13
  113.8 3.6 copy-start.3
  113.8 4.3 %copy-start.7 = (bf16[128,8192]{1,0:T(8,128)(2,1)S(1)}, bf16[128,8192]{1,0:T(8,128)(2,1)}, u32[]{:S(2)}) copy-start(bf16[128,8192]{1,0:T(8,128)(2,1)} %param.9) | copy-start | bytes 6291460
  117.3 2.1 copy-start.2
  126.3 2.1 copy-start
  184.5 178.4 %reduce-scatter.3.cloned.1.call-start = ((), (), s32[]{:S(2)}) async-start(), calls=%async_computation.4 | async-start | bytes 9437184 | tf_op jit(solution)/shard_map/reduce_scatter | solution.py:80
  199.5 4.4 %copy-start.1 = (f32[32,256,128]{2,1,0:T(8,128)S(1)}, f32[32,256,128]{2,1,0:T(8,128)}, u32[]{:S(2)}) copy-start(f32[32,256,128]{2,1,0:T(8,128)} %copy-done) | copy-start | bytes 12582916
  199.6 4.4 %copy-start.5 = (bf16[128,8192]{0,1:T(8,128)(2,1)S(1)}, bf16[128,8192]{0,1:T(8,128)(2,1)}, u32[]{:S(2)}) copy-start(bf16[128,8192]{0,1:T(8,128)(2,1)} %copy-done.4) | copy-start | bytes 6291460
  276.5 48.1 %collective-permute-start.3 = (bf16[128,32,256]{2,0,1:T(8,128)(2,1)}, bf16[128,32,256]{2,0,1:T(8,128)(2,1)}, u32[]{:S(2)}, u32[]{:S(2)}) collective-permute-start(bf16[128,32,256]{2,0,1:T(8,128)(2,1)} %convert_bitcast_fusion), channel_id=1, source_target_pairs={{0,2},{1,3},{2,0},{3,1},{4,6},{5,7},{6,4},{7,5},{8,10},{9,11},{10,... | collective-permute-start | bytes 6291464 | tf_op jit(solution)/shard_map/ppermute | solution.py:13
  279.8 86.3 %collective-permute-start.4 = (bf16[32,1,32,256]{3,2,1,0:T(8,128)(2,1)S(1)}, bf16[32,1,32,256]{3,2,1,0:T(8,128)(2,1)}, u32[]{:S(2)}, u32[]{:S(2)}) collective-permute-start(bf16[32,1,32,256]{3,2,1,0:T(8,128)(2,1)S(1)} %copy.115), channel_id=1, source_target_pairs={{0,1},{1,0},{2,3},{3,2},{4,5},{5,4},{6,7},{7,6},{8,9},{9,8},{10,11... | collective-permute-start | bytes 1572872 | tf_op jit(solution)/shard_map/ppermute | solution.py:13
Sparse Core Ops, SparseCore 0:
  10.3 84.7 all-gather.4
  96.7 80.5 all-gather.2
  184.6 88.0 reduce-scatter.4
  274.9 87.9 reduce-scatter.2
where the time goes:
time: 381 us; the launch traced here: 375 us
  local copies, waits for them, and re-layouts  141 us (37%)
  waiting for transfers between devices  137 us (36%)
  matrix products  45.7 us (12%)
  other arithmetic  27.3 us (7%)
  between operations  14.4 us (4%)
  starting transfers between devices  9.5 us (2%)
    all_gather x1, waiting for transfers between devices, shards(): first_full = lax.all_gather(first_weight, 'dp', axis=2, tiled=True)  55.3 us
    ppermute x5, waiting for transfers between devices, partner(): return lax.ppermute(value, axis, pairs)  55.3 us
    unnamed x25, local copies, waits for them, and re-layouts  26.7 us
    reduce_scatter x1, waiting for transfers between devices, shards(): lax.psum_scatter(first_term.astype(jnp.bfloat16), 'dp', scatter_dimension...  26.7 us
    dot_general x4, matrix products, contract_back(): jnp.einsum('tnj,nkj->tnk', left, right, preferred_element_type=jnp.float32)  21.5 us
    dot_general x2, local copies, waits for them, and re-layouts, outer_sum(): jnp.einsum('tnk,tnj->nkj', left, right, preferred_element_type=jnp.float32)  18.6 us
    gather x2, local copies, waits for them, and re-layouts, shards(): first_cross = jnp.take(outer_sum(partner_in, pre_grad), order_first, axis=1)  17.8 us
    gather x2, local copies, waits for them, and re-layouts, shards(): jnp.take(outer_sum(activated, cot_partner), order_second, axis=1)  17.7 us
  transfers between devices with their start and end apart: 9, of which 4 were waited for; matrix products, arithmetic and copies ran while one was open for 55% of the time, Pallas kernels for 0%

commit v1 on v0

--- a/solution.py
+++ b/solution.py
@@ -1,10 +1,20 @@
+import functools
 import math
 import jax
 import jax.numpy as jnp
 from jax import lax
 from jax.sharding import PartitionSpec as P
+from jax.lax import all_gather
 
 B = 256
+
+
+def review_side_on(a0, bus_axis, join_dim):
+    z_new = jnp.concatenate(all_gather(a0, bus_axis), axis=join_dim)
+    return z_new
+
+
+load_groups = functools.partial(review_side_on, bus_axis="dp", join_dim=2)
 
 
 def partner(value, axis, bit):
@@ -47,7 +57,7 @@
     order_second = orders[1]
     inverse_first = inverse_order(order_first)
     inverse_second = inverse_order(order_second)
-    first_full = lax.all_gather(first_weight, "dp", axis=2, tiled=True)
+    first_full = load_groups(first_weight)
     own_first = first_full[:, 0]
     cross_first = jnp.take(first_full[:, 1], inverse_first, axis=1)
     blocks_in = inputs.reshape(tok_rows, local_blocks, B)

time: 381 us -> 386 us (1.013)
  matrix products: 45.7 us -> 50.2 us
    reshape x0 -> x1, local copies, waits for them, and re-layouts: none -> 8.36 us  [review_side_on(): z_new = jnp.concatenate(all_gather(a0, bus_axis), axis=join_dim)]
    unnamed x25 -> x22, local copies, waits for them, and re-layouts: 26.7 us -> 19.4 us
    squeeze x1 -> x0, local copies, waits for them, and re-layouts: 5.96 us -> none  [shards(): cross_first = jnp.take(first_full[:, 1], inverse_first, axis=1)]
    dot_general x2, matrix products: 8.13 us -> 12 us  [contract(): jnp.einsum('tnk,nkj->tnj', left, right, preferred_element_type=jnp.float32)]
  transfers between devices with their start and end apart: 9 -> 9, of which waited for: 4 -> 4; matrix products, arithmetic and copies ran while one was open for 55% -> 56% of each run, Pallas kernels for 0% -> 0%
where the time goes in v1:
time: 386 us; the launch traced here: 379 us
  local copies, waits for them, and re-layouts  139 us (36%)
  waiting for transfers between devices  139 us (36%)
  matrix products  50.2 us (13%)
  other arithmetic  26.9 us (7%)
  between operations  14.3 us (4%)
  starting transfers between devices  9.08 us (2%)
    all_gather x1, waiting for transfers between devices, review_side_on(): z_new = jnp.concatenate(all_gather(a0, bus_axis), axis=join_dim)  57 us
    ppermute x5, waiting for transfers between devices, partner(): return lax.ppermute(value, axis, pairs)  55.3 us
    reduce_scatter x1, waiting for transfers between devices, shards(): lax.psum_scatter(first_term.astype(jnp.bfloat16), 'dp', scatter_dimension...  25.9 us
    dot_general x4, matrix products, contract_back(): jnp.einsum('tnj,nkj->tnk', left, right, preferred_element_type=jnp.float32)  22.1 us
    unnamed x22, local copies, waits for them, and re-layouts  19.4 us
    dot_general x2, local copies, waits for them, and re-layouts, outer_sum(): jnp.einsum('tnk,tnj->nkj', left, right, preferred_element_type=jnp.float32)  18.6 us
    gather x2, local copies, waits for them, and re-layouts, shards(): first_cross = jnp.take(outer_sum(partner_in, pre_grad), order_first, axis=1)  17.7 us
    gather x2, local copies, waits for them, and re-layouts, shards(): jnp.take(outer_sum(activated, cot_partner), order_second, axis=1)  17.7 us
  transfers between devices with their start and end apart: 9, of which 4 were waited for; matrix products, arithmetic and copies ran while one was open for 56% of the time, Pallas kernels for 0%

profile of v1, /device:TPU:0, one launch (start us, length us, event | category | flops | bytes accessed | tf_op | source)
XLA Modules:
  0.0 378.9 jit_solution(782064770786572341)
XLA Ops:
  12.3 11.9 %collective-permute-done = bf16[32,1,32,256]{3,2,0,1:T(8,128)(2,1)S(1)} collective-permute-done((bf16[32,1,32,256]{3,2,0,1:T(8,128)(2,1)S(1)}, bf16[32,1,32,256]{3,2,0,1:T(8,128)(2,1)S(1)}, u32[]{:S(2)}, u32[]{:S(2)}) %collective-permute-start) | collective-permute-done | bytes 524320 | tf_op jit(solution)/shard_map/ppermute | solution.py:23
  37.4 57.0 %all-gather.6.cloned.1.call-done = bf16[256,2,32,256]{3,2,1,0:T(8,128)(2,1)} async-done(((bf16[32,2,32,256]{3,2,1,0:T(8,128)(2,1)}), bf16[256,2,32,256]{3,2,1,0:T(8,128)(2,1)}) %all-gather.6.cloned.1.call-update) | async-done | bytes 8388624 | tf_op jit(solution)/shard_map/all_gather | solution.py:13
  94.4 8.4 %copy.123 = bf16[32,2,8,32,256]{4,3,2,1,0:T(8,128)(2,1)} copy(bf16[32,2,8,32,256]{4,3,1,0,2:T(8,128)(2,1)} %bitcast.98) | data formatting | bytes 16777216 | tf_op jit(solution)/shard_map/reshape | solution.py:13
  110.3 5.0 %gather_fusion.1 = bf16[256,32,256]{2,1,0:T(8,128)(2,1)} fusion(bf16[32,256,256]{2,0,1:T(8,128)(2,1)} %bitcast.97, s32[1024]{0:T(1024)S(1)} %pad_clamp_fusion.2), kind=kCustom, calls=%fused_computation.2.clone | custom fusion | bytes 8389632 | tf_op jit(solution)/shard_map/jit(_take)/gather | solution.py:62
  118.4 5.2 %fusion.25 = f32[32,256,128]{2,1,0:T(8,128)S(1)} fusion(bf16[32,2,256,256]{3,2,1,0:T(8,128)(2,1)} %bitcast.90, bf16[16,32,8,256]{3,2,1,0:T(8,128)(2,1)S(1)} %bitcast.96), kind=kOutput, calls=%fused_computation.47 | convolution fusion | flops 536870912 | bytes 10485760 | tf_op jit(solution)/shard_map/tnk,nkj->tnj/dot_general | solution.py:38
  123.5 6.9 %fusion.30 = f32[32,256,128]{2,1,0:T(8,128)S(1)} fusion(f32[32,256,128]{2,1,0:T(8,128)S(1)} %fusion.25, bf16[128,32,256]{0,2,1:T(8,128)(2,1)} %bitcast.13, bf16[32,256,256]{2,0,1:T(8,128)(2,1)S(1)} %select_bitcast_fusion.2), kind=kOutput, calls=%fused_computation.55 | convolution fusion | flops 537919488 | bytes 14680064 | tf_op jit(solution)/shard_map/tnk,nkj->tnj/dot_general | solution.py:38
  135.5 8.3 %copy.143 = f32[32,256,256]{2,0,1:T(8,128)} copy(f32[32,256,256]{2,1,0:T(8,128)S(1)} %fusion.39) | data formatting | bytes 16777216 | tf_op jit(solution)/shard_map/tnk,tnj->nkj/dot_general | solution.py:46
  143.8 7.7 %gather_fusion.3 = f32[256,32,256]{2,1,0:T(8,128)} fusion(f32[32,256,256]{2,0,1:T(8,128)} %copy.143, s32[1024]{0:T(1024)S(1)} %pad_clamp_fusion), kind=kCustom, calls=%fused_computation.3.clone | custom fusion | bytes 16778240 | tf_op jit(solution)/shard_map/jit(_take)/gather | solution.py:76
  151.5 10.0 %copy.144 = f32[256,32,256]{0,2,1:T(8,128)} copy(f32[256,32,256]{2,1,0:T(8,128)} %gather_fusion.3) | data formatting | bytes 16777216 | tf_op jit(solution)/shard_map/jit(_take)/gather | solution.py:76
  169.5 4.4 %fusion.1 = bf16[32,2,256,256]{2,3,0,1:T(8,128)(2,1)} fusion(f32[32,1,256,256]{2,3,0,1:T(8,128)S(1)} %select_bitcast_fusion, f32[32,1,256,256]{2,3,0,1:T(8,128)S(1)} %convolution_bitcast_fusion), kind=kLoop, calls=%fused_computation.7 | loop fusion | flops 12582912 | bytes 25165824 | tf_op jit(solution)/shard_map/convert_element_type | solution.py:94
  173.9 14.6 %copy.145 = bf16[32,2,256,256]{3,0,1,2:T(8,128)(2,1)} copy(bf16[32,2,256,256]{2,3,0,1:T(8,128)(2,1)} %fusion.1) | data formatting | bytes 16777216 | tf_op jit(solution)/shard_map/convert_element_type | solution.py:94
  191.3 4.4 %copy.120 = bf16[32,256,256]{2,0,1:T(8,128)(2,1)} copy(bf16[32,256,256]{2,1,0:T(8,128)(2,1)S(1)} %slice_bitcast_fusion.1) | data formatting | bytes 8388608 | tf_op jit(solution)/shard_map/squeeze | solution.py:73
  195.7 5.0 %gather_fusion = bf16[256,32,256]{2,1,0:T(8,128)(2,1)} fusion(bf16[32,256,256]{2,0,1:T(8,128)(2,1)} %copy.120, s32[1024]{0:T(1024)S(1)} %pad_clamp_fusion.3), kind=kCustom, calls=%fused_computation.clone | custom fusion | bytes 8389632 | tf_op jit(solution)/shard_map/jit(_take)/gather | solution.py:73
  208.2 5.8 %fusion.5 = bf16[128,32,256]{0,2,1:T(8,128)(2,1)S(1)} fusion(f32[32,256,128]{2,1,0:T(8,128)S(1)} %copy-done.1, bf16[32,256,128]{2,1,0:T(8,128)(2,1)S(1)} %fusion.22, bf16[128,32,256]{0,2,1:T(8,128)(2,1)S(1)} %bitcast.94, bf16[32,2,256,256]{3,2,0,1:T(8,128)(2,1)} %all-gather.4.cloned.1.call-done), kind=kOutput, calls=%fused_computation.18 | convolution fusion | flops 562036736 | bytes 14680064 | tf_op jit(solution)/shard_map/tnj,nkj->tnk/dot_general | solution.py:42
  213.9 6.1 %convolution_bitcast_fusion.1 = f32[32,256,256]{1,2,0:T(8,128)} fusion(bf16[128,32,256]{0,2,1:T(8,128)(2,1)S(1)} %fusion.5, bf16[128,32,256]{0,2,1:T(8,128)(2,1)} %bitcast.13), kind=kOutput, calls=%fused_computation.53 | convolution fusion | flops 536870912 | bytes 12582912 | tf_op jit(solution)/shard_map/tnk,tnj->nkj/dot_general | solution.py:46
  220.1 10.3 %copy.138 = f32[32,256,256]{2,0,1:T(8,128)} copy(f32[32,256,256]{1,2,0:T(8,128)} %convolution_bitcast_fusion.1) | data formatting | bytes 16777216 | tf_op jit(solution)/shard_map/tnk,tnj->nkj/dot_general | solution.py:46
  230.4 7.8 %gather_fusion.2 = f32[256,32,256]{2,1,0:T(8,128)} fusion(f32[32,256,256]{2,0,1:T(8,128)} %copy.138, s32[1024]{0:T(1024)S(1)} %pad_clamp_fusion.1), kind=kCustom, calls=%fused_computation.1.clone | custom fusion | bytes 16778240 | tf_op jit(solution)/shard_map/jit(_take)/gather | solution.py:87
  238.2 9.9 %copy.139 = f32[256,32,256]{0,2,1:T(8,128)} copy(f32[256,32,256]{2,1,0:T(8,128)} %gather_fusion.2) | data formatting | bytes 16777216 | tf_op jit(solution)/shard_map/jit(_take)/gather | solution.py:87
  255.0 4.4 %fusion = bf16[32,2,256,256]{2,3,0,1:T(8,128)(2,1)} fusion(f32[32,1,256,256]{2,3,0,1:T(8,128)S(1)} %select_bitcast_fusion.1, f32[32,1,256,256]{2,3,0,1:T(8,128)S(1)} %convolution_bitcast_fusion.2), kind=kLoop, calls=%fused_computation.5 | loop fusion | flops 12582912 | bytes 25165824 | tf_op jit(solution)/shard_map/convert_element_type | solution.py:91
  259.4 14.9 %copy.140 = bf16[32,2,256,256]{3,0,1,2:T(8,128)(2,1)} copy(bf16[32,2,256,256]{2,3,0,1:T(8,128)(2,1)} %fusion) | data formatting | bytes 16777216 | tf_op jit(solution)/shard_map/convert_element_type | solution.py:91
  274.3 6.2 %convert_bitcast_fusion = bf16[128,32,256]{2,0,1:T(8,128)(2,1)} fusion(bf16[128,32,256]{0,2,1:T(8,128)(2,1)S(1)} %fusion.5, bf16[32,256,256]{2,0,1:T(8,128)(2,1)} %copy-done.2), kind=kOutput, calls=%fused_computation.58 | convolution fusion | flops 537919488 | bytes 8388608 | tf_op jit(solution)/shard_map/tnj,nkj->tnk/dot_general | solution.py:42
  285.0 43.4 %collective-permute-done.3 = bf16[128,32,256]{2,0,1:T(8,128)(2,1)} collective-permute-done((bf16[128,32,256]{2,0,1:T(8,128)(2,1)}, bf16[128,32,256]{2,0,1:T(8,128)(2,1)}, u32[]{:S(2)}, u32[]{:S(2)}) %collective-permute-start.3) | collective-permute-done | bytes 2097184 | tf_op jit(solution)/shard_map/ppermute | solution.py:23
  328.4 5.8 %fusion.20 = bf16[128,32,256]{2,0,1:T(8,128)(2,1)} fusion(bf16[128,32,256]{2,0,1:T(8,128)(2,1)} %collective-permute-done.3, bf16[128,32,256]{0,2,1:T(8,128)(2,1)S(1)} %fusion.5, bf16[32,2,256,256]{3,2,1,0:T(8,128)(2,1)} %bitcast.91), kind=kOutput, calls=%fused_computation.38 | convolution fusion | flops 540016640 | bytes 10485760 | tf_op jit(solution)/shard_map/tnj,nkj->tnk/dot_general | solution.py:42
  340.6 25.9 %reduce-scatter.3.cloned.1.call-done = bf16[32,2,32,256]{3,0,1,2:T(8,128)(2,1)} async-done(((bf16[32,2,256,256]{3,0,1,2:T(8,128)(2,1)}), bf16[32,2,32,256]{3,0,1,2:T(8,128)(2,1)}) %reduce-scatter.3.cloned.1.call-update) | async-done | bytes 1048592 | tf_op jit(solution)/shard_map/reduce_scatter | solution.py:90
  (72 shorter events, 75.4 us)
Async XLA Ops:
  7.2 18.2 %copy-start.5 = (bf16[128,8192]{1,0:T(8,128)(2,1)S(1)}, bf16[128,8192]{1,0:T(8,128)(2,1)}, u32[]{:S(2)}) copy-start(bf16[128,8192]{1,0:T(8,128)(2,1)} %param.9) | copy-start | bytes 6291460
  7.2 87.2 %all-gather.6.cloned.1.call-start = ((), (), s32[]{:S(2)}) async-start(), calls=%async_computation.5 | async-start | bytes 9437184 | tf_op jit(solution)/shard_map/all_gather | solution.py:13
  7.9 180.9 %all-gather.4.cloned.1.call-start = ((), (), s32[]{:S(2)}) async-start(), calls=%async_computation.2 | async-start | bytes 9437184 | tf_op jit(solution)/shard_map/all_gather | solution.py:71
  9.2 15.0 %collective-permute-start = (bf16[32,1,32,256]{3,2,0,1:T(8,128)(2,1)S(1)}, bf16[32,1,32,256]{3,2,0,1:T(8,128)(2,1)S(1)}, u32[]{:S(2)}, u32[]{:S(2)}) collective-permute-start(bf16[32,1,32,256]{3,2,0,1:T(8,128)(2,1)S(1)} %get-tuple-element.23), channel_id=1, source_target_pairs={{0,1},{1,0},{2,3},{3,2},{4,5},{5,4},{6,7},{7,6},{8,9},{9,8},{10,11... | collective-permute-start | bytes 1572872 | tf_op jit(solution)/shard_map/ppermute | solution.py:23
  25.3 256.6 %reduce-scatter.5.cloned.1.call-start = ((), (), s32[]{:S(2)}) async-start(), calls=%async_computation.4 | async-start | bytes 9437184 | tf_op jit(solution)/shard_map/reduce_scatter | solution.py:93
  27.8 9.4 %copy-start.7 = (s32[2,256]{1,0:T(2,128)S(1)}, s32[2,256]{1,0:T(2,128)}, u32[]{:S(2)}) copy-start(s32[2,256]{1,0:T(2,128)} %param.13) | copy-start | bytes 6148
  27.8 95.7 %collective-permute-start.2 = (bf16[128,8192]{0,1:T(8,128)(2,1)}, bf16[128,8192]{0,1:T(8,128)(2,1)}, u32[]{:S(2)}, u32[]{:S(2)}) collective-permute-start(bf16[128,8192]{0,1:T(8,128)(2,1)} %copy.127), channel_id=1, source_target_pairs={{0,2},{1,3},{2,0},{3,1},{4,6},{5,7},{6,4},{7,5},{8,10},{9,11},{10,... | collective-permute-start | bytes 6291464 | tf_op jit(solution)/shard_map/ppermute | solution.py:23
  32.8 128.7 %copy-start.3 = (bf16[128,8192]{0,1:T(8,128)(2,1)}, bf16[128,8192]{0,1:T(8,128)(2,1)S(1)}, u32[]{:S(2)}) copy-start(bf16[128,8192]{0,1:T(8,128)(2,1)S(1)} %copy.118) | copy-start | bytes 6291460
  35.7 94.7 %collective-permute-start.1 = (bf16[128,32,256]{2,0,1:T(8,128)(2,1)}, bf16[128,32,256]{2,0,1:T(8,128)(2,1)}, u32[]{:S(2)}, u32[]{:S(2)}) collective-permute-start(bf16[128,32,256]{2,0,1:T(8,128)(2,1)} %copy.121), channel_id=1, source_target_pairs={{0,1},{1,0},{2,3},{3,2},{4,5},{5,4},{6,7},{7,6},{8,9},{9,8},{10,11... | collective-permute-start | bytes 6291464 | tf_op jit(solution)/shard_map/ppermute | solution.py:23
  115.3 3.1 copy-start.6
  118.3 5.2 %copy-start.2 = (bf16[32,256,256]{2,0,1:T(8,128)(2,1)}, bf16[32,256,256]{2,0,1:T(8,128)(2,1)S(1)}, u32[]{:S(2)}) copy-start(bf16[32,256,256]{2,0,1:T(8,128)(2,1)S(1)} %select_bitcast_fusion.2) | copy-start | bytes 12582916
  130.4 2.0 copy-start
  188.6 177.9 %reduce-scatter.3.cloned.1.call-start = ((), (), s32[]{:S(2)}) async-start(), calls=%async_computation.3 | async-start | bytes 9437184 | tf_op jit(solution)/shard_map/reduce_scatter | solution.py:90
  203.8 4.4 %copy-start.1 = (f32[32,256,128]{2,1,0:T(8,128)S(1)}, f32[32,256,128]{2,1,0:T(8,128)}, u32[]{:S(2)}) copy-start(f32[32,256,128]{2,1,0:T(8,128)} %copy-done) | copy-start | bytes 12582916
  203.8 4.4 %copy-start.4 = (bf16[128,8192]{0,1:T(8,128)(2,1)S(1)}, bf16[128,8192]{0,1:T(8,128)(2,1)}, u32[]{:S(2)}) copy-start(bf16[128,8192]{0,1:T(8,128)(2,1)} %copy-done.3) | copy-start | bytes 6291460
  280.5 47.8 %collective-permute-start.3 = (bf16[128,32,256]{2,0,1:T(8,128)(2,1)}, bf16[128,32,256]{2,0,1:T(8,128)(2,1)}, u32[]{:S(2)}, u32[]{:S(2)}) collective-permute-start(bf16[128,32,256]{2,0,1:T(8,128)(2,1)} %convert_bitcast_fusion), channel_id=1, source_target_pairs={{0,2},{1,3},{2,0},{3,1},{4,6},{5,7},{6,4},{7,5},{8,10},{9,11},{10,... | collective-permute-start | bytes 6291464 | tf_op jit(solution)/shard_map/ppermute | solution.py:23
  283.7 85.9 %collective-permute-start.4 = (bf16[32,1,32,256]{3,2,1,0:T(8,128)(2,1)S(1)}, bf16[32,1,32,256]{3,2,1,0:T(8,128)(2,1)}, u32[]{:S(2)}, u32[]{:S(2)}) collective-permute-start(bf16[32,1,32,256]{3,2,1,0:T(8,128)(2,1)S(1)} %copy.146), channel_id=1, source_target_pairs={{0,1},{1,0},{2,3},{3,2},{4,5},{5,4},{6,7},{7,6},{8,9},{9,8},{10,11... | collective-permute-start | bytes 1572872 | tf_op jit(solution)/shard_map/ppermute | solution.py:23
Sparse Core Ops, SparseCore 0:
  9.6 84.7 all-gather.5
  96.0 80.5 all-gather.3
  188.7 87.5 reduce-scatter.4
  278.5 87.9 reduce-scatter.2
